TPU v7x, 256 devices: a whole 4x4x8 slice. The times are simulated.
256 devices in a mesh: dp: 4 (over x_lo, core), seq: 64 (over x_hi, z, y).
Axes of the slice: x: 4 (x_hi: 2, x_lo: 2; x = x_hi * 2 + x_lo), y: 4, z: 8, core: 2. Of those that a mesh axis runs over, the one named last changes fastest.
Arguments:
- hidden: bfloat16 [4, 8192, 2048], P('dp', 'seq'), may hold values from -16 to 16
- tokens: int32 [4, 8192], P('dp', 'seq'), may hold values from 0 to 4
- embedding: float32 [5, 2048], replicated, may hold values from -6 to 6
- weight: bfloat16 [2048, 1024], P('dp'), may hold values from -0.125 to 0.125
- kernel: float32 [7, 1024], replicated, may hold values from -2.4 to 2.4
- cotangent: bfloat16 [4, 8192, 1024], P('dp', 'seq'), may hold values from -6 to 6
Outputs:
- block_result: bfloat16 [4, 8192, 1024], P('dp', 'seq')
- grad_hidden: bfloat16 [4, 8192, 2048], P('dp', 'seq')
- grad_weight: float32 [2048, 1024], P('dp')
- grad_kernel: float32 [7, 1024], replicated
- grad_embedding: float32 [5, 2048], replicated
All inputs are finite; a program needn't handle non-finite values.
Results may differ from a plain program's by a relative error of at most 0.0095.
Values may be sent and summed in bfloat16 or wider, within the bound.
No kernel may reach another device: no remote copies, remote signals or barrier semaphores. Data moves between devices by JAX's collectives and lax.ppermute only.
A program may use at most 64 MiB of HBM per device.

v0:
```python
import math
import jax
import jax.numpy as jnp
from jax import lax
from jax.sharding import PartitionSpec as P


def padded_2(cells, sides, width):
    for axis, dim in sides:
        count = lax.axis_size(axis)
        ends = count - 1
        head = lax.slice_in_dim(cells, 0, width, axis=dim)
        tail = lax.slice_in_dim(cells, cells.shape[dim] - width, cells.shape[dim], axis=dim)
        cells = jnp.concatenate(
            [
                lax.ppermute(tail, axis, [(i, (i + 1) % count) for i in range(ends)]),
                cells,
                lax.ppermute(head, axis, [((i + 1) % count, i) for i in range(ends)]),
            ],
            axis=dim,
        )
    return cells


def mirror_rows(conv_block):
    device_list = lax.axis_size("seq")
    row_count = conv_block.shape[0]
    column_names = conv_block.shape[1]
    window_slab_rows = row_count // device_list
    slab_split = conv_block.reshape(device_list, 1, window_slab_rows, column_names)
    spread_out = lax.all_to_all(slab_split, "seq", split_axis=0, concat_axis=1, tiled=True)
    turned = spread_out[0, ::-1].reshape(device_list, 1, window_slab_rows, column_names)
    second = lax.all_to_all(turned, "seq", split_axis=0, concat_axis=1, tiled=True)
    return second.reshape(row_count, column_names)[::-1]


def local(hidden, tokens, embedding, weight, kernel, cotangent):
    window = hidden[0]
    token_codes = tokens[0]
    upstream = cotangent[0]
    row_count = window.shape[0]
    features = window.shape[1]
    tap_count = kernel.shape[0]
    margin = (tap_count - 1) // 2
    positions = hidden.shape[0] * row_count * lax.axis_size("dp") * lax.axis_size("seq")
    factor = 1.0 / math.sqrt(positions)
    one_hot = (
        jnp.arange(embedding.shape[0], dtype=jnp.int32)[:, None] == token_codes[None, :]
    ).astype(jnp.float32)
    looked = lax.dot_general(
        one_hot,
        embedding,
        (((0,), (0,)), ((), ())),
        precision=lax.Precision.HIGHEST,
        preferred_element_type=jnp.float32,
    )
    stream = (window.astype(jnp.float32) + looked).astype(jnp.bfloat16)
    mirrored = mirror_rows(jnp.concatenate([stream, upstream], axis=1))
    stream_rev = mirrored[:, :features][:, ::-1]
    upstream_rev = mirrored[:, features:][:, ::-1]
    kernels = jnp.stack([kernel, kernel])
    stacked = jnp.concatenate([stream, stream_rev], axis=0)
    column_names = stacked
    projected = jnp.dot(
        column_names,
        lax.all_gather(weight, "dp", axis=0, tiled=True),
        preferred_element_type=jnp.float32,
    )
    forward_part = projected[:row_count]
    reverse_part = projected[row_count:]
    values = jnp.stack([forward_part, reverse_part]).astype(jnp.bfloat16)
    padded = padded_2(values, (("seq", 1),), margin)
    widened = padded.astype(jnp.float32)
    mixing = kernels[:, 0][:, None, :] * widened[:, 0:row_count]
    for tap_index in range(1, tap_count):
        mixing = (
            mixing
            + kernels[:, tap_index][:, None, :] * widened[:, tap_index : tap_index + row_count]
        )
    linear = values.astype(jnp.float32)
    logistic = jax.nn.sigmoid(linear)
    gating = linear * logistic
    strands = mixing * gating
    reverse_out = strands[1].astype(jnp.bfloat16)
    returned = mirror_rows(reverse_out)[:, ::-1]
    block_result = (strands[0] + returned.astype(jnp.float32)).astype(jnp.bfloat16)
    upstreams = jnp.stack([upstream, upstream_rev]).astype(jnp.float32)
    grad_mix = upstreams * gating
    accumulated = upstreams * mixing * logistic * (1.0 + linear * (1.0 - logistic))
    grad_padded = padded_2(grad_mix, (("seq", 1),), margin)
    for tap_index in range(tap_count):
        lower = 2 * margin - tap_index
        accumulated = (
            accumulated
            + kernels[:, tap_index][:, None, :] * grad_padded[:, lower : lower + row_count]
        )
    grad_values = accumulated.astype(jnp.bfloat16)
    kernel_terms = jnp.stack(
        [
            jnp.sum(grad_mix * widened[:, tap_index : tap_index + row_count], axis=1)
            for tap_index in range(tap_count)
        ],
        axis=1,
    )
    kernel_part = kernel_terms[0] + kernel_terms[1]
    grad_reverse = grad_values[1]
    grad_stack = jnp.concatenate([grad_values[0], grad_reverse], axis=0)
    column_names = stacked
    owner_rows = lax.psum_scatter(
        lax.dot_general(
            column_names, grad_stack, (((0,), (0,)), ((), ())), preferred_element_type=jnp.float32
        ).astype(jnp.bfloat16),
        "dp",
        scatter_dimension=0,
        tiled=True,
    ).astype(jnp.float32)
    grad_weight = lax.psum(owner_rows, "seq") * factor
    back_stack = lax.dot_general(
        grad_stack,
        lax.all_gather(weight, "dp", axis=0, tiled=True),
        (((1,), (1,)), ((), ())),
        preferred_element_type=jnp.float32,
    )
    reverse_back = back_stack[row_count:].astype(jnp.bfloat16)
    reverse_back = mirror_rows(reverse_back)[:, ::-1]
    grad_stream = back_stack[:row_count] + reverse_back.astype(jnp.float32)
    table_part = jnp.dot(
        one_hot, grad_stream, precision=lax.Precision.HIGHEST, preferred_element_type=jnp.float32
    )
    kernel_sum, table_sum = lax.psum((kernel_part, table_part), ("dp", "seq"))
    return (
        block_result[None],
        grad_stream.astype(jnp.bfloat16)[None],
        grad_weight,
        kernel_sum * factor,
        table_sum * factor,
    )


def solution(mesh):
    in_specs = (P("dp", "seq", None), P("dp", "seq"), P(), P("dp", None), P(), P("dp", "seq", None))
    out_specs = (P("dp", "seq", None), P("dp", "seq", None), P("dp", None), P(), P())
    return jax.shard_map(local, mesh=mesh, in_specs=in_specs, out_specs=out_specs, check_vma=False)
```

profile of v0, /device:TPU:2, one launch (start us, length us, event | category | flops | bytes accessed | tf_op | source)
XLA Modules:
  0.0 851.3 jit_solution(7686276310235606197)
XLA Ops:
  7.2 0.7 all-gather.2.cloned.1.call-update
  7.9 1.1 concatenate.29
  9.0 1.7 fusion
  10.7 0.3 concatenate.28
  11.0 0.7 pad_maximum_fusion.3
  11.7 38.0 %all_to_all.63 = bf16[64,1,2,3072]{3,2,1,0:T(2,128)(2,1)S(1)} all-to-all(bf16[64,1,2,3072]{3,2,1,0:T(2,128)(2,1)S(1)} %pad_maximum_fusion.3), channel_id=1, replica_groups=mesh['dp'=4,'seq'=64] {'seq'}, dimensions={0} | all-to-all | bytes 1572864 | tf_op jit(solution)/shard_map/all_to_all | solution.py:31
  49.7 1.4 reverse_bitcast_fusion
  51.2 6.2 all-to-all-start.1
  57.4 23.5 %all-to-all-done.1 = bf16[64,1,2,3072]{3,2,1,0:T(2,128)(2,1)S(1)} async-done(((bf16[64,1,2,3072]{3,2,1,0:T(2,128)(2,1)}), bf16[64,1,2,3072]{3,2,1,0:T(2,128)(2,1)S(1)}, u32[]{:S(2)}, u32[]{:S(2)}) %all-to-all-start.1) | async-done | bytes 786464 | tf_op jit(solution)/shard_map/all_to_all | solution.py:33
  80.9 0.3 reshape.62
  81.2 5.8 rev.25
  87.0 3.6 convolution_convert_fusion.1
  90.7 2.4 collective-permute-start
  93.1 1.3 collective-permute-start.1
  94.4 0.9 rev.28
  95.3 3.4 collective-permute-done.1
  98.7 0.2 maximum_convert_fusion
  98.9 1.3 multiply_reduce_fusion
  100.3 1.3 collective-permute-start.2
  101.6 4.7 collective-permute-start.3
  106.3 1.5 collective-permute-done.3
  107.9 2.4 fusion.5
  110.3 1.3 fusion.31
  111.7 1.3 copy-done.1
  113.1 0.3 reshape.64
  113.4 36.5 %all_to_all.64 = bf16[64,1,2,2048]{3,2,1,0:T(2,128)(2,1)S(1)} all-to-all(bf16[64,1,2,2048]{3,2,1,0:T(2,128)(2,1)S(1)} %bitcast.68), channel_id=1, replica_groups=mesh['dp'=4,'seq'=64] {'seq'}, dimensions={0} | all-to-all | bytes 1048576 | tf_op jit(solution)/shard_map/all_to_all | solution.py:31
  149.9 1.2 reverse_bitcast_fusion.1
  151.0 5.7 all-to-all-start.5
  157.0 0.6 fusion.33
  157.6 14.2 %all-to-all-done.5 = bf16[64,1,2,2048]{3,2,1,0:T(2,128)(2,1)S(1)} async-done(((bf16[64,1,2,2048]{3,2,1,0:T(2,128)(2,1)}), bf16[64,1,2,2048]{3,2,1,0:T(2,128)(2,1)S(1)}, u32[]{:S(2)}, u32[]{:S(2)}) %all-to-all-start.5) | async-done | bytes 524320 | tf_op jit(solution)/shard_map/all_to_all | solution.py:33
  171.9 0.2 reshape.65
  172.1 1.8 rev.30
  173.9 2.4 fusion.25
  176.3 4.3 convolution_convert_fusion
  180.7 0.3 fusion.30
  181.0 0.1 convert_element_type.58
  181.1 18.9 %all_to_all.65 = bf16[64,1,2,1024]{3,2,1,0:T(2,128)(2,1)S(1)} all-to-all(bf16[64,1,2,1024]{3,2,1,0:T(2,128)(2,1)S(1)} %bitcast.70), channel_id=1, replica_groups=mesh['dp'=4,'seq'=64] {'seq'}, dimensions={0} | all-to-all | bytes 524288 | tf_op jit(solution)/shard_map/all_to_all | solution.py:31
  200.0 0.2 reverse_bitcast_fusion.2
  200.2 18.0 %all_to_all.66 = bf16[64,1,2,1024]{3,2,1,0:T(2,128)(2,1)S(1)} all-to-all(bf16[64,1,2,1024]{3,2,1,0:T(2,128)(2,1)S(1)} %reverse_bitcast_fusion.2), channel_id=1, replica_groups=mesh['dp'=4,'seq'=64] {'seq'}, dimensions={0} | all-to-all | bytes 524288 | tf_op jit(solution)/shard_map/all_to_all | solution.py:33
  218.3 0.9 rev.27
  219.2 0.8 fusion.32
  220.0 2.1 fusion.27
  222.1 194.8 %all-reduce.4.cloned.1.call-done = (f32[7,1024]{1,0:T(8,128)}, f32[5,2048]{1,0:T(8,128)}) async-done(((f32[7,1024]{1,0:T(8,128)}, f32[5,2048]{1,0:T(8,128)}), (f32[7,1024]{1,0:T(8,128)}, f32[5,2048]{1,0:T(8,128)})) %all-reduce.4.cloned.1.call-update) | async-done | bytes 69648 | tf_op jit(solution)/shard_map/psum | solution.py:130
  416.9 1.4 broadcast_multiply_fusion.2
  418.3 1.5 broadcast_multiply_fusion.1
  419.8 42.5 %reduce-scatter.2.cloned.1.call-done = bf16[512,1024]{1,0:T(8,128)(2,1)} async-done(((bf16[2048,1024]{1,0:T(8,128)(2,1)}), bf16[512,1024]{1,0:T(8,128)(2,1)}) %reduce-scatter.2.cloned.1.call-update) | async-done | bytes 1048592 | tf_op jit(solution)/shard_map/reduce_scatter | solution.py:109
  462.3 380.9 %all-reduce.5 = f32[512,1024]{1,0:T(8,128)S(1)} all-reduce(bf16[512,1024]{1,0:T(8,128)(2,1)} %reduce-scatter.2.cloned.1.call-done), channel_id=1, replica_groups=mesh['dp'=4,'seq'=64] {'seq'}, use_global_device_ids=true, to_apply=%region_1.0 | all-reduce | flops 524288 | bytes 3145728 | tf_op jit(solution)/shard_map/psum | solution.py:117
  843.2 1.5 broadcast_multiply_fusion
  (43 shorter events, 0.8 us)
Async XLA Ops:
  7.2 1.8 copy-start
  7.2 79.8 %all-gather.2.cloned.1.call-start = ((), (), s32[]{:S(2)}) async-start(), calls=%async_computation.7 | async-start | bytes 5242880 | tf_op jit(solution)/shard_map/all_gather | solution.py:66
  11.7 45.6 %copy-start.4 = (f32[7,1024]{1,0:T(8,128)S(1)}, f32[7,1024]{1,0:T(8,128)}, u32[]{:S(2)}) copy-start(f32[7,1024]{1,0:T(8,128)} %param.10) | copy-start | bytes 86020
  51.2 29.7 %all-to-all-start.1 = ((bf16[64,1,2,3072]{3,2,1,0:T(2,128)(2,1)}), bf16[64,1,2,3072]{3,2,1,0:T(2,128)(2,1)S(1)}, u32[]{:S(2)}, u32[]{:S(2)}) async-start(bf16[64,1,2,3072]{3,2,1,0:T(2,128)(2,1)} %reverse_bitcast_fusion), calls=%async_computation.1 | async-start | bytes 1572864 | tf_op jit(solution)/shard_map/all_to_all | solution.py:33
  90.6 8.3 copy-start.2
  90.7 4.6 collective-permute-start
  93.1 5.6 collective-permute-start.1
  100.3 6.1 collective-permute-start.2
  101.6 6.3 collective-permute-start.3
  107.9 2.4 copy-start.6
  110.3 1.4 copy-start.3
  111.7 1.3 copy-start.1
  149.9 24.0 %copy-start.5 = (s32[1,128]{1,0:T(1,128)S(1)}, s32[1,128]{1,0:T(1,128)}, u32[]{:S(2)}) copy-start(s32[1,128]{1,0:T(1,128)} %param.7) | copy-start | bytes 1540
  151.0 20.8 %all-to-all-start.5 = ((bf16[64,1,2,2048]{3,2,1,0:T(2,128)(2,1)}), bf16[64,1,2,2048]{3,2,1,0:T(2,128)(2,1)S(1)}, u32[]{:S(2)}, u32[]{:S(2)}) async-start(bf16[64,1,2,2048]{3,2,1,0:T(2,128)(2,1)} %reverse_bitcast_fusion.1), calls=%async_computation.5 | async-start | bytes 1048576 | tf_op jit(solution)/shard_map/all_to_all | solution.py:33
  156.7 260.2 %all-reduce.4.cloned.1.call-start = ((), (), s32[]{:S(2)}) async-start(), calls=%async_computation.9 | async-start | bytes 196608 | tf_op jit(solution)/shard_map/psum | solution.py:130
  176.2 286.0 %reduce-scatter.2.cloned.1.call-start = ((), (), s32[]{:S(2)}) async-start(), calls=%async_computation.8 | async-start | bytes 5242880 | tf_op jit(solution)/shard_map/reduce_scatter | solution.py:109
Sparse Core Ops, SparseCore 0:
  9.8 66.1 all-gather.1
  176.4 240.5 all-reduce.3
  419.5 42.7 reduce-scatter.1
where the time goes:
time: 852 us; the launch traced here: 851 us
  blocking collectives  492 us (58%)
  waiting for transfers between devices  281 us (33%)
  starting transfers between devices  21.7 us (3%)
  local copies, waits for them, and re-layouts  16.3 us (2%)
  between operations  14.2 us (2%)
  matrix products  13.4 us (2%)
  other arithmetic  12.8 us (2%)
    psum x1, blocking collectives, local(): grad_weight = lax.psum(owner_rows, 'seq') * factor  381 us
    psum x1, waiting for transfers between devices, local(): kernel_sum, table_sum = lax.psum((kernel_part, table_part), ('dp', 'seq'))  195 us
    all_to_all x3, blocking collectives, mirror_rows(): lax.all_to_all(slab_split, 'seq', split_axis=0, concat_axis=1, tiled=True)  93.4 us
    reduce_scatter x1, waiting for transfers between devices, local(): lax.psum_scatter(lax.dot_general(column_names, grad_stack, (((0,), (0,)),...  42.5 us
    all_to_all x2, waiting for transfers between devices, mirror_rows(): lax.all_to_all(turned, 'seq', split_axis=0, concat_axis=1, tiled=True)  37.7 us
    all_to_all x1, blocking collectives, mirror_rows(): lax.all_to_all(turned, 'seq', split_axis=0, concat_axis=1, tiled=True)  18 us
  transfers between devices with their start and end apart: 9, of which 6 were waited for; matrix products, arithmetic and copies ran while one was open for 3% of the time, Pallas kernels for 0%

commit v1 on v0

--- a/solution.py
+++ b/solution.py
@@ -127,7 +127,7 @@
     table_part = jnp.dot(
         one_hot, grad_stream, precision=lax.Precision.HIGHEST, preferred_element_type=jnp.float32
     )
-    kernel_sum, table_sum = lax.psum((kernel_part, table_part), ("dp", "seq"))
+    kernel_sum, table_sum = lax.psum(lax.psum((kernel_part, table_part), "seq"), "dp")
     return (
         block_result[None],
         grad_stream.astype(jnp.bfloat16)[None],

time: 852 us -> 638 us (0.75)
  waiting for transfers between devices: 281 us -> 99.1 us
  blocking collectives: 492 us -> 417 us
  starting transfers between devices: 21.7 us -> 55.3 us
    psum x1, waiting for transfers between devices: 195 us -> 33.1 us  [local(): lax.psum(lax.psum((kernel_part, table_part), 'seq'), 'dp')]
    all_to_all x3 -> x1, blocking collectives: 93.4 us -> 38 us  [mirror_rows(): lax.all_to_all(slab_split, 'seq', split_axis=0, concat_axis=1, tiled=True)]
    reduce_scatter x1, waiting for transfers between devices: 42.5 us -> 0.01 us  [local(): lax.psum_scatter(lax.dot_general(column_names, grad_stack, (((0,), (0,)),...]
    all_to_all x0 -> x2, starting transfers between devices: none -> 28 us  [mirror_rows(): lax.all_to_all(slab_split, 'seq', split_axis=0, concat_axis=1, tiled=True)]
    all_to_all x0 -> x2, waiting for transfers between devices: none -> 20.5 us  [mirror_rows(): lax.all_to_all(slab_split, 'seq', split_axis=0, concat_axis=1, tiled=True)]
    all_to_all x1 -> x0, blocking collectives: 18 us -> none  [mirror_rows(): lax.all_to_all(turned, 'seq', split_axis=0, concat_axis=1, tiled=True)]
    all_to_all x2 -> x3, starting transfers between devices: 11.9 us -> 17.5 us  [mirror_rows(): lax.all_to_all(turned, 'seq', split_axis=0, concat_axis=1, tiled=True)]
    all_to_all x2 -> x3, waiting for transfers between devices: 37.7 us -> 39.8 us  [mirror_rows(): lax.all_to_all(turned, 'seq', split_axis=0, concat_axis=1, tiled=True)]
  transfers between devices with their start and end apart: 9 -> 12, of which waited for: 6 -> 8; matrix products, arithmetic and copies ran while one was open for 3% -> 5% of each run, Pallas kernels for 0% -> 0%
where the time goes in v1:
time: 638 us; the launch traced here: 634 us
  blocking collectives  417 us (65%)
  waiting for transfers between devices  99.1 us (16%)
  starting transfers between devices  55.3 us (9%)
  local copies, waits for them, and re-layouts  24.2 us (4%)
  between operations  14.2 us (2%)
  matrix products  12.6 us (2%)
  other arithmetic  11.6 us (2%)
    psum x1, blocking collectives, local(): grad_weight = lax.psum(owner_rows, 'seq') * factor  379 us
    all_to_all x3, waiting for transfers between devices, mirror_rows(): lax.all_to_all(turned, 'seq', split_axis=0, concat_axis=1, tiled=True)  39.8 us
    all_to_all x1, blocking collectives, mirror_rows(): lax.all_to_all(slab_split, 'seq', split_axis=0, concat_axis=1, tiled=True)  38 us
    psum x1, waiting for transfers between devices, local(): lax.psum(lax.psum((kernel_part, table_part), 'seq'), 'dp')  33.1 us
    all_to_all x2, starting transfers between devices, mirror_rows(): lax.all_to_all(slab_split, 'seq', split_axis=0, concat_axis=1, tiled=True)  28 us
    all_to_all x2, waiting for transfers between devices, mirror_rows(): lax.all_to_all(slab_split, 'seq', split_axis=0, concat_axis=1, tiled=True)  20.5 us
    all_to_all x3, starting transfers between devices, mirror_rows(): lax.all_to_all(turned, 'seq', split_axis=0, concat_axis=1, tiled=True)  17.5 us
  transfers between devices with their start and end apart: 12, of which 8 were waited for; matrix products, arithmetic and copies ran while one was open for 5% of the time, Pallas kernels for 0%

profile of v1, /device:TPU:2, one launch (start us, length us, event | category | flops | bytes accessed | tf_op | source)
XLA Modules:
  0.0 634.0 jit_solution(1323244700072091173)
XLA Ops:
  7.2 0.7 all-gather.2.cloned.1.call-update
  7.9 1.1 concatenate.29
  9.0 1.7 fusion
  11.0 0.7 pad_maximum_fusion.3
  11.7 38.0 %all_to_all.63 = bf16[64,1,2,3072]{3,2,1,0:T(2,128)(2,1)S(1)} all-to-all(bf16[64,1,2,3072]{3,2,1,0:T(2,128)(2,1)S(1)} %pad_maximum_fusion.3), channel_id=1, replica_groups=mesh['dp'=4,'seq'=64] {'seq'}, dimensions={0} | all-to-all | bytes 1572864 | tf_op jit(solution)/shard_map/all_to_all | solution.py:31
  49.7 1.4 reverse_bitcast_fusion
  51.2 6.2 all-to-all-start.1
  57.5 23.4 %all-to-all-done.1 = bf16[64,1,2,3072]{3,2,1,0:T(2,128)(2,1)S(1)} async-done(((bf16[64,1,2,3072]{3,2,1,0:T(2,128)(2,1)}), bf16[64,1,2,3072]{3,2,1,0:T(2,128)(2,1)S(1)}, u32[]{:S(2)}, u32[]{:S(2)}) %all-to-all-start.1) | async-done | bytes 786464 | tf_op jit(solution)/shard_map/all_to_all | solution.py:33
  81.2 1.8 rev.25
  83.0 3.4 convolution_convert_fusion.1
  86.5 2.4 collective-permute-start
  88.9 1.3 collective-permute-start.1
  90.3 0.9 rev.28
  91.2 3.4 collective-permute-done.1
  94.7 1.3 multiply_reduce_fusion
  96.1 1.3 collective-permute-start.2
  97.4 4.7 collective-permute-start.3
  102.2 1.5 collective-permute-done.3
  103.7 2.4 fusion.5
  106.1 3.2 convolution_convert_fusion
  109.7 0.8 convert_element_type.58
  110.5 21.6 %all-to-all-start.2 = ((bf16[64,1,2,1024]{3,2,1,0:T(2,128)(2,1)}), bf16[64,1,2,1024]{3,2,1,0:T(2,128)(2,1)S(1)}, u32[]{:S(2)}, u32[]{:S(2)}) async-start(bf16[64,1,2,1024]{3,2,1,0:T(2,128)(2,1)} %bitcast.10), calls=%async_computation.2 | async-start | bytes 524288 | tf_op jit(solution)/shard_map/all_to_all | solution.py:31
  132.2 3.7 fusion.31
  135.9 0.9 slice.306
  136.8 2.2 reshape.64
  138.9 6.5 %all-to-all-done.2 = bf16[64,1,2,1024]{3,2,1,0:T(2,128)(2,1)S(1)} async-done(((bf16[64,1,2,1024]{3,2,1,0:T(2,128)(2,1)}), bf16[64,1,2,1024]{3,2,1,0:T(2,128)(2,1)S(1)}, u32[]{:S(2)}, u32[]{:S(2)}) %all-to-all-start.2) | async-done | bytes 262176 | tf_op jit(solution)/shard_map/all_to_all | solution.py:31
  145.4 6.3 all-to-all-start.4
  151.8 0.9 reverse_bitcast_fusion.2
  152.7 14.0 %all-to-all-done.4 = bf16[64,1,2,2048]{3,2,1,0:T(2,128)(2,1)} async-done(((bf16[64,1,2,2048]{3,2,1,0:T(2,128)(2,1)}), bf16[64,1,2,2048]{3,2,1,0:T(2,128)(2,1)}, u32[]{:S(2)}, u32[]{:S(2)}) %all-to-all-start.4) | async-done | bytes 524320 | tf_op jit(solution)/shard_map/all_to_all | solution.py:31
  166.7 5.9 all-to-all-start.3
  172.5 2.2 reverse_bitcast_fusion.1
  174.7 11.2 %all-to-all-done.3 = bf16[64,1,2,1024]{3,2,1,0:T(2,128)(2,1)S(1)} async-done(((bf16[64,1,2,1024]{3,2,1,0:T(2,128)(2,1)}), bf16[64,1,2,1024]{3,2,1,0:T(2,128)(2,1)S(1)}, u32[]{:S(2)}, u32[]{:S(2)}) %all-to-all-start.3) | async-done | bytes 262176 | tf_op jit(solution)/shard_map/all_to_all | solution.py:33
  185.9 5.5 all-to-all-start.5
  191.5 0.6 stack.59
  194.5 0.9 stack.63
  195.3 0.6 fusion.33
  196.0 0.8 reshape.63
  196.8 3.5 rev.27
  200.3 0.8 fusion.32
  201.1 5.3 all-to-all-done.5
  206.4 1.2 reshape.65
  207.6 1.8 rev.30
  209.9 0.9 fusion.27
  210.8 379.1 %all-reduce.6 = (f32[512,1024]{1,0:T(8,128)S(1)}, f32[7,1024]{1,0:T(8,128)}, f32[5,2048]{1,0:T(8,128)}) all-reduce(bf16[512,1024]{1,0:T(8,128)(2,1)} %reduce-scatter.2.cloned.1.call-done, f32[7,1024]{1,0:T(8,128)S(1)} %copy-done.4, f32[5,2048]{1,0:T(8,128)S(1)} %fusion.25), channel_id=1, replica_groups=mesh['dp'=4,'seq'=64] {'seq'}, use_global_device_ids=true, to_apply=%region_1.0 | all-reduce | flops 541696 | bytes 3284992 | tf_op jit(solution)/shard_map/psum | solution.py:117
  590.0 1.5 broadcast_multiply_fusion
  591.5 33.1 %all-reduce.5.cloned.1.call-done = (f32[7,1024]{1,0:T(8,128)}, f32[5,2048]{1,0:T(8,128)}) async-done(((f32[7,1024]{1,0:T(8,128)}, f32[5,2048]{1,0:T(8,128)}), (f32[7,1024]{1,0:T(8,128)}, f32[5,2048]{1,0:T(8,128)})) %all-reduce.5.cloned.1.call-update) | async-done | bytes 69648 | tf_op jit(solution)/shard_map/psum | solution.py:130
  624.6 1.4 broadcast_multiply_fusion.2
  626.0 1.5 broadcast_multiply_fusion.1
  (46 shorter events, 4.5 us)
Async XLA Ops:
  7.2 1.8 copy-start
  7.2 75.8 %all-gather.2.cloned.1.call-start = ((), (), s32[]{:S(2)}) async-start(), calls=%async_computation.7 | async-start | bytes 5242880 | tf_op jit(solution)/shard_map/all_gather | solution.py:66
  11.7 45.6 %copy-start.5 = (f32[7,1024]{1,0:T(8,128)S(1)}, f32[7,1024]{1,0:T(8,128)}, u32[]{:S(2)}) copy-start(f32[7,1024]{1,0:T(8,128)} %param.10) | copy-start | bytes 86020
  51.2 29.7 %all-to-all-start.1 = ((bf16[64,1,2,3072]{3,2,1,0:T(2,128)(2,1)}), bf16[64,1,2,3072]{3,2,1,0:T(2,128)(2,1)S(1)}, u32[]{:S(2)}, u32[]{:S(2)}) async-start(bf16[64,1,2,3072]{3,2,1,0:T(2,128)(2,1)} %reverse_bitcast_fusion), calls=%async_computation.1 | async-start | bytes 1572864 | tf_op jit(solution)/shard_map/all_to_all | solution.py:33
  57.3 153.5 %reduce-scatter.2.cloned.1.call-start = ((), (), s32[]{:S(2)}) async-start(), calls=%async_computation.8 | async-start | bytes 5242880 | tf_op jit(solution)/shard_map/reduce_scatter | solution.py:109
  86.5 8.3 %copy-start.1 = (bf16[1,128,1024]{2,1,0:T(8,128)(2,1)S(1)}, bf16[1,128,1024]{2,1,0:T(8,128)(2,1)}, u32[]{:S(2)}) copy-start(bf16[1,128,1024]{2,1,0:T(8,128)(2,1)} %param.11) | copy-start | bytes 786436
  86.5 4.6 collective-permute-start
  88.9 5.6 collective-permute-start.1
  96.1 6.1 collective-permute-start.2
  97.4 6.3 collective-permute-start.3
  106.1 3.3 copy-start.2
  106.1 3.3 copy-start.3
  110.5 34.9 %all-to-all-start.2 = ((bf16[64,1,2,1024]{3,2,1,0:T(2,128)(2,1)}), bf16[64,1,2,1024]{3,2,1,0:T(2,128)(2,1)S(1)}, u32[]{:S(2)}, u32[]{:S(2)}) async-start(bf16[64,1,2,1024]{3,2,1,0:T(2,128)(2,1)} %bitcast.10), calls=%async_computation.2 | async-start | bytes 524288 | tf_op jit(solution)/shard_map/all_to_all | solution.py:31
  145.4 21.2 %all-to-all-start.4 = ((bf16[64,1,2,2048]{3,2,1,0:T(2,128)(2,1)}), bf16[64,1,2,2048]{3,2,1,0:T(2,128)(2,1)}, u32[]{:S(2)}, u32[]{:S(2)}) async-start(bf16[64,1,2,2048]{3,2,1,0:T(2,128)(2,1)} %bitcast.68), calls=%async_computation.4 | async-start | bytes 1048576 | tf_op jit(solution)/shard_map/all_to_all | solution.py:31
  166.7 19.2 %all-to-all-start.3 = ((bf16[64,1,2,1024]{3,2,1,0:T(2,128)(2,1)}), bf16[64,1,2,1024]{3,2,1,0:T(2,128)(2,1)S(1)}, u32[]{:S(2)}, u32[]{:S(2)}) async-start(bf16[64,1,2,1024]{3,2,1,0:T(2,128)(2,1)} %reverse_bitcast_fusion.2), calls=%async_computation.3 | async-start | bytes 524288 | tf_op jit(solution)/shard_map/all_to_all | solution.py:33
  185.9 20.5 %all-to-all-start.5 = ((bf16[64,1,2,2048]{3,2,1,0:T(2,128)(2,1)}), bf16[64,1,2,2048]{3,2,1,0:T(2,128)(2,1)}, u32[]{:S(2)}, u32[]{:S(2)}) async-start(bf16[64,1,2,2048]{3,2,1,0:T(2,128)(2,1)} %reverse_bitcast_fusion.1), calls=%async_computation.5 | async-start | bytes 1048576 | tf_op jit(solution)/shard_map/all_to_all | solution.py:33
  191.4 433.2 %all-reduce.5.cloned.1.call-start = ((), (), s32[]{:S(2)}) async-start(), calls=%async_computation.9 | async-start | bytes 196608 | tf_op jit(solution)/shard_map/psum | solution.py:130
  196.0 13.4 %copy-start.6 = (s32[1,128]{1,0:T(1,128)S(1)}, s32[1,128]{1,0:T(1,128)}, u32[]{:S(2)}) copy-start(s32[1,128]{1,0:T(1,128)} %param.7) | copy-start | bytes 1540
  209.4 1.4 copy-start.4
Sparse Core Ops, SparseCore 0:
  9.8 66.1 all-gather.1
  109.5 65.7 reduce-scatter.1
  590.1 34.4 all-reduce.4
